TPU v7x, 32 devices: a whole 2x2x4 slice. The times are simulated.
32 devices in a mesh: dp: 8 (over y, x, core), tensor: 4 (over z).
Axes of the slice: x: 2, y: 2, z: 4, core: 2. Of those that a mesh axis runs over, the one named last changes fastest.
Arguments:
- acts: bfloat16 [8192, 256], P('dp'), may hold values from -6 to 6
- out_grad: bfloat16 [8192, 4096], P('dp', 'tensor'), may hold values from -6 to 6
- weight: float32 [256, 4096], P(None, 'tensor'), may hold values from -0.375 to 0.375
- error: float32 [8, 256, 4096], P('dp', None, 'tensor'), may hold values from -6 to 6
- start_q: float32 [4096, 64], P('tensor'), may hold values from -0.1875 to 0.1875
Outputs:
- new_weight: float32 [256, 4096], P(None, 'tensor')
- new_error: float32 [8, 256, 4096], P('dp', None, 'tensor')
- input_grad: float32 [8192, 256], P(('dp', 'tensor'))
All inputs are finite; a program needn't handle non-finite values.
Results may differ from a plain program's by a relative error of at most 0.0003.
Values sent between devices are 32-bit elements; how exact they have to be, the bound alone decides.
No kernel may reach another device: no remote copies, remote signals or barrier semaphores. Data moves between devices by JAX's collectives and lax.ppermute only.
A program may use at most 64 MiB of HBM per device.

v0:
```python
import math

import jax
import jax.numpy as jnp
from jax import lax
from jax.sharding import PartitionSpec as P

HIGH = lax.Precision.HIGHEST


def local(acts, out_grad, weight, error, start_q):
    tok_rows = acts.shape[0]
    replicas = lax.axis_size("dp")
    gradient = jnp.einsum(
        "td,tc->dc", acts, out_grad, preferred_element_type=jnp.float32
    ) / math.sqrt(tok_rows)
    merged = gradient + error[0]
    left = lax.psum(jnp.dot(merged, start_q, precision=HIGH), "dp") / replicas
    gram = jnp.dot(left.T, left, precision=HIGH)
    chol = jnp.linalg.cholesky(gram)
    ortho = jax.scipy.linalg.solve_triangular(chol, left.T, lower=True).T
    right = lax.psum(jnp.dot(merged.T, ortho, precision=HIGH), "dp") / replicas
    delta = jnp.dot(ortho, right.T, precision=HIGH)
    new_error = (merged - delta)[None]
    new_weight = weight - delta
    partial_sum = jnp.dot(out_grad.astype(jnp.float32), weight.T, precision=HIGH)
    input_grad = lax.psum_scatter(partial_sum, "tensor", scatter_dimension=0, tiled=True)
    return (new_weight, new_error, input_grad)


def solution(mesh):
    placed = (
        P("dp", None),
        P("dp", "tensor"),
        P(None, "tensor"),
        P("dp", None, "tensor"),
        P("tensor", None),
    )
    return jax.shard_map(
        local,
        mesh=mesh,
        in_specs=placed,
        out_specs=(P(None, "tensor"), P("dp", None, "tensor"), P(("dp", "tensor"), None)),
        check_vma=False,
    )
```

profile of v0, /device:TPU:0, one launch (start us, length us, event | category | flops | bytes accessed | tf_op | source)
XLA Modules:
  0.0 152.2 jit_solution(6092948681229038225)
XLA Ops:
  8.0 0.0 copy-start
  8.0 0.0 copy-start.1
  8.0 0.0 all-reduce.3.cloned.1.call-start
  8.1 1.5 %copy-done = bf16[1024,1024]{1,0:T(8,128)(2,1)S(1)} copy-done((bf16[1024,1024]{1,0:T(8,128)(2,1)S(1)}, bf16[1024,1024]{1,0:T(8,128)(2,1)}, u32[]{:S(2)}) %copy-start) | copy-done | bytes 2097176
  9.6 2.1 %fusion = f32[256,1024]{1,0:T(8,128)S(1)} fusion(bf16[1024,256]{1,0:T(8,128)(2,1)} %param.5, bf16[1024,1024]{1,0:T(8,128)(2,1)S(1)} %copy-done, f32[1,256,1024]{2,1,0:T(8,128)} %param.8), kind=kOutput, calls=%fused_computation.1 | convolution fusion | flops 537395200 | bytes 4718592 | tf_op jit(solution)/shard_map/td,tc->dc/dot_general | solution.py:14
  11.7 0.0 copy-done.1
  11.7 1.7 %fusion.18 = f32[256,64]{0,1:T(8,128)} fusion(f32[256,1024]{1,0:T(8,128)S(1)} %fusion, f32[1024,64]{0,1:T(8,128)S(1)} %copy-done.1), kind=kOutput, calls=%fused_computation.24 | convolution fusion | flops 201326592 | bytes 1376256 | tf_op jit(solution)/shard_map/dot_general | solution.py:18
  13.5 0.0 all-reduce.3.cloned.1.call-update
  13.5 0.0 all-reduce.5.cloned.1.call-start
  13.5 56.0 %all-reduce.3.cloned.1.call-done = f32[256,64]{0,1:T(8,128)} async-done(((f32[256,64]{0,1:T(8,128)}), f32[256,64]{0,1:T(8,128)}) %all-reduce.3.cloned.1.call-update) | async-done | bytes 65552 | tf_op jit(solution)/shard_map/psum | solution.py:18
  69.5 1.1 fusion.6
  70.7 0.1 copy.8
  70.8 5.8 %cholesky.16 = f32[64,64]{1,0:T(8,128)S(1)} custom-call(f32[64,64]{1,0:T(8,128)S(1)} %fusion.10), custom_call_target="Cholesky" | custom-call | tf_op jit(solution)/shard_map/jit(cholesky)/cholesky | solution.py:20
  76.6 0.6 compare_reduce_fusion
  77.3 0.7 fusion.8
  77.9 4.9 %custom-call.7 = f32[1,64,64]{1,2,0:T(8,128)S(1)} custom-call(f32[1,64,64]{2,1,0:T(8,128)S(1)} %fusion.8), custom_call_target="InvertDiagBlocksLowerTriangular" | custom-call | tf_op jit(solution)/shard_map/jit(_solve_triangular)/triangular_solve | solution.py:21
  82.8 1.1 fusion.4
  84.0 2.6 %fusion.19 = f32[1024,64]{1,0:T(8,128)} fusion(f32[256,1024]{1,0:T(8,128)S(1)} %fusion, f32[64,256]{1,0:T(8,128)S(1)} %fusion.4), kind=kOutput, calls=%fused_computation.25 | convolution fusion | flops 201326592 | bytes 1376256 | tf_op jit(solution)/shard_map/dot_general | solution.py:22
  86.6 0.0 all-reduce.5.cloned.1.call-update
  86.6 0.0 reduce-scatter.2.cloned.1.call-start
  86.6 4.1 %fusion.20 = f32[1024,256]{1,0:T(8,128)} fusion(bf16[1024,1024]{1,0:T(8,128)(2,1)S(1)} %copy-done, f32[256,1024]{1,0:T(8,128)} %param.7), kind=kOutput, calls=%fused_computation.26 | convolution fusion | flops 3221225472 | bytes 4194304 | tf_op jit(solution)/shard_map/dot_general | solution.py:26
  90.7 0.0 reduce-scatter.2.cloned.1.call-update
  90.7 50.2 %all-reduce.5.cloned.1.call-done = f32[1024,64]{1,0:T(8,128)} async-done(((f32[1024,64]{1,0:T(8,128)}), f32[1024,64]{1,0:T(8,128)}) %all-reduce.5.cloned.1.call-update) | async-done | bytes 262160 | tf_op jit(solution)/shard_map/psum | solution.py:22
  140.9 3.8 %subtract_bitcast_fusion = (f32[1,256,1024]{2,1,0:T(8,128)}, f32[256,1024]{1,0:T(8,128)}) fusion(f32[256,1024]{1,0:T(8,128)S(1)} %fusion, f32[256,1024]{1,0:T(8,128)} %param.7, f32[64,256]{1,0:T(8,128)S(1)} %fusion.4, f32[1024,64]{1,0:T(8,128)} %all-reduce.5.cloned.1.call-done), kind=kOutput, calls=%fused_computation.2 | convolution fusion | flops 201916416 | bytes 4521984 | tf_op jit(solution)/shard_map/dot_general | solution.py:23
  144.7 0.0 reduce-scatter.2.cloned.1.call-done
  (2 shorter events, 0.0 us)
Async XLA Ops:
  8.0 1.6 %copy-start = (bf16[1024,1024]{1,0:T(8,128)(2,1)S(1)}, bf16[1024,1024]{1,0:T(8,128)(2,1)}, u32[]{:S(2)}) copy-start(bf16[1024,1024]{1,0:T(8,128)(2,1)} %param.6) | copy-start | bytes 6291460
  8.0 3.7 %copy-start.1 = (f32[1024,64]{0,1:T(8,128)S(1)}, f32[1024,64]{0,1:T(8,128)}, u32[]{:S(2)}) copy-start(f32[1024,64]{0,1:T(8,128)} %param.9) | copy-start | bytes 786436
  8.0 61.5 %all-reduce.3.cloned.1.call-start = ((), (), s32[]{:S(2)}) async-start(), calls=%async_computation.1 | async-start | bytes 131072 | tf_op jit(solution)/shard_map/psum | solution.py:18
  13.5 127.5 %all-reduce.5.cloned.1.call-start = ((), (), s32[]{:S(2)}) async-start(), calls=%async_computation.2 | async-start | bytes 1048576 | tf_op jit(solution)/shard_map/psum | solution.py:22
  86.6 58.2 %reduce-scatter.2.cloned.1.call-start = ((), (), s32[]{:S(2)}) async-start(), calls=%async_computation.3 | async-start | bytes 1310720 | tf_op jit(solution)/shard_map/reduce_scatter | solution.py:27
Sparse Core Ops, SparseCore 0:
  13.6 55.8 all-reduce.2
  86.7 54.1 all-reduce.4
Sparse Core Ops, SparseCore 1:
  90.8 26.6 reduce-scatter.1
where the time goes:
time: 153 us; the launch traced here: 152 us
  waiting for transfers between devices  106 us (69%)
  matrix products  16.5 us (11%)
  between operations  15.6 us (10%)
  other arithmetic  12.1 us (8%)
  local copies, waits for them, and re-layouts  1.61 us (1%)
    psum x1, waiting for transfers between devices, local(): left = lax.psum(jnp.dot(merged, start_q, precision=HIGH), 'dp') / replicas  56 us
    psum x1, waiting for transfers between devices, local(): right = lax.psum(jnp.dot(merged.T, ortho, precision=HIGH), 'dp') / replicas  50.2 us
    another operation x3, other arithmetic, local(): chol = jnp.linalg.cholesky(gram)  6.52 us
    another operation x2, other arithmetic, local(): ortho = jax.scipy.linalg.solve_triangular(chol, left.T, lower=True).T  5.55 us
    dot_general x1, matrix products, local(): jnp.dot(out_grad.astype(jnp.float32), weight.T, precision=HIGH)  4.08 us
    dot_general x1, matrix products, local(): delta = jnp.dot(ortho, right.T, precision=HIGH)  3.79 us
  transfers between devices with their start and end apart: 3, of which 2 were waited for; matrix products, arithmetic and copies ran while one was open for 5% of the time, Pallas kernels for 0%

commit v1 on v0

v1 whole, which is shorter than its diff:
```python
import math

import jax
import jax.numpy as jnp
from jax import lax
from jax.sharding import PartitionSpec as P

HIGH = lax.Precision.HIGH


def flip(bit_even, bit_odd, size):
    return [(i, i ^ (bit_odd if i & 1 else bit_even)) for i in range(size)]


def local(acts, out_grad, weight, error, start_q):
    tok_rows = acts.shape[0]
    din, cols = weight.shape
    replicas = lax.axis_size("dp")
    n_tensor = lax.axis_size("tensor")
    half = cols // 2
    side = lax.axis_index("dp") % 2
    t_idx = lax.axis_index("tensor")
    bits = [1 << b for b in range(1, replicas.bit_length() - 1)]

    gradient = jnp.einsum(
        "td,tc->dc", acts, out_grad, preferred_element_type=jnp.float32
    ) / math.sqrt(tok_rows)
    merged = gradient + error[0]
    left = lax.dot_general(start_q, merged, (((0,), (1,)), ((), ())), precision=HIGH)

    mine = lax.dynamic_slice(merged, (0, side * half), (din, half))
    theirs = lax.dynamic_slice(merged, (0, (1 - side) * half), (din, half))
    pair = flip(1, 1, replicas)
    left = left + lax.ppermute(left, "dp", pair)
    total = mine + lax.ppermute(theirs, "dp", pair)

    partial_sum = jnp.dot(out_grad.astype(jnp.float32), weight.T, precision=HIGH)
    block = tok_rows // n_tensor

    def rows(k):
        return lax.dynamic_slice(partial_sum, (((t_idx + k) % n_tensor) * block, 0), (block, din))

    input_grad = rows(0)
    for k in range(1, n_tensor):
        input_grad = input_grad + lax.ppermute(
            rows(k), "tensor", [(i, (i + k) % n_tensor) for i in range(n_tensor)]
        )

    for even, odd in zip(bits, bits[::-1]):
        swap = flip(even, odd, replicas)
        left = left + lax.ppermute(left, "dp", flip(even, even, replicas))
        total = total + lax.ppermute(total, "dp", swap)
    left = left / replicas
    gram = lax.dot_general(left, left, (((1,), (1,)), ((), ())), precision=lax.Precision.HIGHEST)
    chol = jnp.linalg.cholesky(gram)
    ortho = jax.scipy.linalg.solve_triangular(chol, left, lower=True)
    right = jnp.dot(ortho, total, precision=HIGH) / replicas
    other = lax.ppermute(right, "dp", pair)
    right = jnp.where(side == 0, jnp.concatenate([right, other], 1), jnp.concatenate([other, right], 1))
    delta = lax.dot_general(ortho, right, (((0,), (0,)), ((), ())), precision=HIGH)
    return (weight - delta, (merged - delta)[None], input_grad)


def solution(mesh):
    placed = (
        P("dp", None),
        P("dp", "tensor"),
        P(None, "tensor"),
        P("dp", None, "tensor"),
        P("tensor", None),
    )
    return jax.shard_map(
        local,
        mesh=mesh,
        in_specs=placed,
        out_specs=(P(None, "tensor"), P("dp", None, "tensor"), P(("dp", "tensor"), None)),
        check_vma=False,
    )
```

time: 153 us -> 50.7 us (0.33)
  waiting for transfers between devices: 106 us -> 1.53 us
  between operations: 15.6 us -> 0.77 us
  starting transfers between devices: 0.12 us -> 12.8 us
  other arithmetic: 12.1 us -> 20.2 us
  matrix products: 16.5 us -> 9.88 us
  local copies, waits for them, and re-layouts: 1.61 us -> 5.09 us
    psum x2 -> x0, waiting for transfers between devices: 106 us -> none  [the longest x1 56 us: local(): left = lax.psum(jnp.dot(merged, start_q, precision=HIGH), 'dp') / replicas]
    ppermute x0 -> x10, starting transfers between devices: none -> 12.8 us  [the longest x3 5.51 us: local(): lax.ppermute(rows(k), 'tensor', [(i, (i + k) % n_tensor) for i in range(n...]
    add x0 -> x5, other arithmetic: none -> 6.81 us  [the longest x1 2.07 us: local(): total = total + lax.ppermute(total, 'dp', swap)]
    dot_general x4, matrix products: 9.22 us -> 4.29 us  [the longest x1 1.99 us: local(): lax.dot_general(ortho, right, (((0,), (0,)), ((), ())), precision=HIGH)]
    dynamic_slice x0 -> x2, local copies, waits for them, and re-layouts: none -> 2.8 us  [the longest x1 1.96 us: rows(): lax.dynamic_slice(partial_sum, ((t_idx + k) % n_tensor * block, 0), (bloc...]
    dot_general x1, matrix products: 4.08 us -> 2.26 us  [local(): jnp.dot(out_grad.astype(jnp.float32), weight.T, precision=HIGH)]
  transfers between devices with their start and end apart: 3 -> 10, of which waited for: 2 -> 3; matrix products, arithmetic and copies ran while one was open for 5% -> 56% of each run, Pallas kernels for 0% -> 0%
where the time goes in v1:
time: 50.7 us; the launch traced here: 50.2 us
  other arithmetic  20.2 us (40%)
  starting transfers between devices  12.8 us (25%)
  matrix products  9.88 us (19%)
  local copies, waits for them, and re-layouts  5.09 us (10%)
  waiting for transfers between devices  1.53 us (3%)
  between operations  0.77 us (2%)
    another operation x3, other arithmetic, local(): chol = jnp.linalg.cholesky(gram)  7.28 us
    ppermute x3, starting transfers between devices, local(): lax.ppermute(rows(k), 'tensor', [(i, (i + k) % n_tensor) for i in range(n...  5.51 us
    another operation x2, other arithmetic, local(): ortho = jax.scipy.linalg.solve_triangular(chol, left, lower=True)  5.48 us
    ppermute x2, starting transfers between devices, local(): left = left + lax.ppermute(left, 'dp', flip(even, even, replicas))  4.62 us
    dot_general x1, matrix products, local(): jnp.dot(out_grad.astype(jnp.float32), weight.T, precision=HIGH)  2.26 us
    unnamed x10, local copies, waits for them, and re-layouts  2.21 us
    dot_general x1, matrix products, local(): jnp.einsum('td,tc->dc', acts, out_grad, preferred_element_type=jnp.float32)  2.15 us
    add x1, other arithmetic, local(): total = total + lax.ppermute(total, 'dp', swap)  2.07 us
  transfers between devices with their start and end apart: 10, of which 3 were waited for; matrix products, arithmetic and copies ran while one was open for 56% of the time, Pallas kernels for 0%

profile of v1, /device:TPU:0, one launch (start us, length us, event | category | flops | bytes accessed | tf_op | source)
XLA Modules:
  0.0 50.2 jit_solution(7805031549578826171)
XLA Ops:
  0.6 0.0 copy-start
  0.7 1.6 %copy-done = bf16[1024,1024]{1,0:T(8,128)(2,1)S(1)} copy-done((bf16[1024,1024]{1,0:T(8,128)(2,1)S(1)}, bf16[1024,1024]{1,0:T(8,128)(2,1)}, u32[]{:S(2)}) %copy-start) | copy-done | bytes 2097176
  2.2 0.0 copy-start.4
  2.2 2.2 %fusion = f32[256,1024]{1,0:T(8,128)S(1)} fusion(bf16[1024,256]{1,0:T(8,128)(2,1)} %param.5, bf16[1024,1024]{1,0:T(8,128)(2,1)S(1)} %copy-done, f32[1,256,1024]{2,1,0:T(8,128)} %param.8), kind=kOutput, calls=%fused_computation.1 | convolution fusion | flops 537395200 | bytes 4718592 | tf_op jit(solution)/shard_map/td,tc->dc/dot_general | solution.py:25
  4.4 0.0 copy-start.1
  4.4 0.8 %constant_dynamic-slice_fusion.3 = f32[256,512]{1,0:T(8,128)} fusion(f32[256,1024]{1,0:T(8,128)S(1)} %fusion, s32[]{:T(128)S(6)} %select_n.57), kind=kLoop, calls=%fused_computation.31 | loop fusion | bytes 1048580 | tf_op jit(solution)/shard_map/dynamic_slice | solution.py:32
  5.2 0.5 collective-permute-start.3
  5.7 0.0 copy-done.4
  5.7 0.6 %convolution_bitcast_fusion = f32[64,256]{1,0:T(8,128)S(1)} fusion(f32[256,1024]{1,0:T(8,128)S(1)} %fusion, f32[1024,64]{0,1:T(8,128)S(1)} %copy-done.4), kind=kOutput, calls=%fused_computation.3 | convolution fusion | flops 100663296 | bytes 1376256 | tf_op jit(solution)/shard_map/dot_general | solution.py:29
  6.3 0.1 collective-permute-start
  6.4 0.0 copy-done.1
  6.4 2.3 %fusion.17 = f32[1024,256]{1,0:T(8,128)} fusion(bf16[1024,1024]{1,0:T(8,128)(2,1)S(1)} %copy-done, f32[256,1024]{1,0:T(8,128)S(1)} %copy-done.1), kind=kOutput, calls=%fused_computation.35 | convolution fusion | flops 1610612736 | bytes 4194304 | tf_op jit(solution)/shard_map/dot_general | solution.py:37
  8.7 0.0 collective-permute-done
  8.7 3.0 %collective-permute-start.1 = (f32[64,256]{1,0:T(8,128)S(1)}, f32[64,256]{1,0:T(8,128)}, u32[]{:S(2)}, u32[]{:S(2)}) collective-permute-start(f32[64,256]{1,0:T(8,128)S(1)} %add.86), channel_id=1, source_target_pairs={{0,8},{4,12},{8,0},{12,4},{16,24},{20,28},{24,16},{28,20},{1,9},{5... | collective-permute-start | bytes 196616 | tf_op jit(solution)/shard_map/ppermute | solution.py:51
  11.7 2.0 %constant_dynamic-slice_fusion.2 = (f32[256,256]{1,0:T(8,128)}, f32[256,256]{1,0:T(8,128)S(1)}, f32[256,256]{1,0:T(8,128)}) fusion(f32[1024,256]{1,0:T(8,128)} %fusion.17, s32[]{:T(128)S(6)} %select_n.62, s32[]{:T(128)S(6)} %select_n.66, s32[]{:T(128)S(6)} %select_n.64), kind=kLoop, calls=%fused_computation.30 | loop fusion | bytes 1572876 | tf_op jit(solution)/shard_map/dynamic_slice | solution.py:41
  13.7 1.6 %collective-permute-start.7 = (f32[256,256]{1,0:T(8,128)}, f32[256,256]{1,0:T(8,128)}, u32[]{:S(2)}, u32[]{:S(2)}) collective-permute-start(f32[256,256]{1,0:T(8,128)} %get-tuple-element.3), channel_id=1, source_target_pairs={{0,1},{1,2},{2,3},{3,0},{4,5},{5,6},{6,7},{7,4},{8,9},{9,10},{10,1... | collective-permute-start | bytes 786440 | tf_op jit(solution)/shard_map/ppermute | solution.py:45
  15.3 2.6 %collective-permute-start.8 = (f32[256,256]{1,0:T(8,128)}, f32[256,256]{1,0:T(8,128)}, u32[]{:S(2)}, u32[]{:S(2)}) collective-permute-start(f32[256,256]{1,0:T(8,128)} %get-tuple-element.5), channel_id=1, source_target_pairs={{0,2},{1,3},{2,0},{3,1},{4,6},{5,7},{6,4},{7,5},{8,10},{9,11},{10,... | collective-permute-start | bytes 786440 | tf_op jit(solution)/shard_map/ppermute | solution.py:45
  17.9 1.3 %collective-permute-start.9 = (f32[256,256]{1,0:T(8,128)S(1)}, f32[256,256]{1,0:T(8,128)}, u32[]{:S(2)}, u32[]{:S(2)}) collective-permute-start(f32[256,256]{1,0:T(8,128)S(1)} %get-tuple-element.4), channel_id=1, source_target_pairs={{0,3},{1,0},{2,1},{3,2},{4,7},{5,4},{6,5},{7,6},{8,11},{9,8},{10,9... | collective-permute-start | bytes 786440 | tf_op jit(solution)/shard_map/ppermute | solution.py:45
  19.2 0.0 collective-permute-done.1
  19.2 0.8 %add.87 = f32[64,256]{1,0:T(8,128)S(1)} add(f32[64,256]{1,0:T(8,128)S(1)} %add.86, f32[64,256]{1,0:T(8,128)} %collective-permute-done.1) | non-fusion elementwise | flops 16384 | bytes 196608 | tf_op jit(solution)/shard_map/add | solution.py:51
  20.1 1.6 %collective-permute-start.2 = (f32[64,256]{1,0:T(8,128)S(1)}, f32[64,256]{1,0:T(8,128)S(1)}, u32[]{:S(2)}, u32[]{:S(2)}) collective-permute-start(f32[64,256]{1,0:T(8,128)S(1)} %add.87), channel_id=1, source_target_pairs={{0,16},{4,20},{8,24},{12,28},{16,0},{20,4},{24,8},{28,12},{1,17},{... | collective-permute-start | bytes 196616 | tf_op jit(solution)/shard_map/ppermute | solution.py:51
  21.7 0.0 collective-permute-done.3
  21.7 1.9 %dynamic-slice_add_fusion = f32[256,512]{1,0:T(8,128)} fusion(f32[256,512]{1,0:T(8,128)} %collective-permute-done.3, f32[256,1024]{1,0:T(8,128)S(1)} %fusion, s32[]{:T(128)S(6)} %select_n.56), kind=kLoop, calls=%fused_computation.6 | loop fusion | flops 131072 | bytes 1572868 | tf_op jit(solution)/shard_map/add | solution.py:35
  23.6 0.5 %collective-permute-start.4 = (f32[256,512]{1,0:T(8,128)}, f32[256,512]{1,0:T(8,128)}, u32[]{:S(2)}, u32[]{:S(2)}) collective-permute-start(f32[256,512]{1,0:T(8,128)} %dynamic-slice_add_fusion), channel_id=1, source_target_pairs={{0,8},{4,20},{8,0},{12,28},{16,24},{20,4},{24,16},{28,12},{1,9},{5... | collective-permute-start | bytes 1572872 | tf_op jit(solution)/shard_map/ppermute | solution.py:52
  24.1 0.3 collective-permute-done.2
  24.4 0.6 %copy-done.3 = f32[64,256]{1,0:T(8,128)} copy-done((f32[64,256]{1,0:T(8,128)}, f32[64,256]{1,0:T(8,128)S(1)}, u32[]{:S(2)}) %copy-start.3) | copy-done | bytes 65560
  25.0 0.2 fusion.13
  25.2 0.1 copy.8
  25.3 0.6 %fusion.12 = f32[64,64]{1,0:T(8,128)} fusion(f32[64,64]{1,0:T(8,128)S(1)} %fusion.13, f32[64,64]{0,1:T(8,128)S(1)} %copy.8), kind=kLoop, calls=%fused_computation.22 | loop fusion | flops 8192 | bytes 49152 | tf_op jit(solution)/shard_map/jit(cholesky)/div | solution.py:55
  25.9 6.6 %cholesky.16 = f32[64,64]{1,0:T(8,128)S(1)} custom-call(f32[64,64]{1,0:T(8,128)} %fusion.12), custom_call_target="Cholesky" | custom-call | tf_op jit(solution)/shard_map/jit(cholesky)/cholesky | solution.py:55
  32.6 0.5 %collective-permute-done.4 = f32[256,512]{1,0:T(8,128)} collective-permute-done((f32[256,512]{1,0:T(8,128)}, f32[256,512]{1,0:T(8,128)}, u32[]{:S(2)}, u32[]{:S(2)}) %collective-permute-start.4) | collective-permute-done | bytes 524320 | tf_op jit(solution)/shard_map/ppermute | solution.py:52
  33.1 2.1 %add.94 = f32[256,512]{1,0:T(8,128)} add(f32[256,512]{1,0:T(8,128)} %dynamic-slice_add_fusion, f32[256,512]{1,0:T(8,128)} %collective-permute-done.4) | non-fusion elementwise | flops 131072 | bytes 1572864 | tf_op jit(solution)/shard_map/add | solution.py:52
  35.1 1.4 %collective-permute-start.5 = (f32[256,512]{1,0:T(8,128)}, f32[256,512]{1,0:T(8,128)}, u32[]{:S(2)}, u32[]{:S(2)}) collective-permute-start(f32[256,512]{1,0:T(8,128)} %add.94), channel_id=1, source_target_pairs={{0,16},{4,12},{8,24},{12,4},{16,0},{20,28},{24,8},{28,20},{1,17},{... | collective-permute-start | bytes 1572872 | tf_op jit(solution)/shard_map/ppermute | solution.py:52
  36.6 0.6 %compare_reduce_fusion = pred[]{:T(512)} fusion(f32[64]{0:T(128)S(1)} %select_reduce_fusion), kind=kLoop, calls=%fused_computation.27 | loop fusion | flops 127 | bytes 257 | tf_op jit(solution)/shard_map/jit(cholesky)/cholesky | solution.py:55
  37.2 0.6 %fusion.9 = f32[1,64,64]{2,1,0:T(8,128)S(1)} fusion(f32[64,64]{1,0:T(8,128)S(1)} %cholesky.16, pred[]{:T(512)} %compare_reduce_fusion), kind=kLoop, calls=%fused_computation.18 | loop fusion | flops 16384 | bytes 32769 | tf_op jit(solution)/shard_map/jit(_solve_triangular)/triangular_solve | solution.py:56
  37.8 4.9 %custom-call.7 = f32[1,64,64]{1,2,0:T(8,128)S(1)} custom-call(f32[1,64,64]{2,1,0:T(8,128)S(1)} %fusion.9), custom_call_target="InvertDiagBlocksLowerTriangular" | custom-call | tf_op jit(solution)/shard_map/jit(_solve_triangular)/triangular_solve | solution.py:56
  42.7 0.0 copy-start.2
  42.7 1.2 %fusion.10 = f32[64,256]{1,0:T(8,128)S(1)} fusion(f32[1,64,64]{1,2,0:T(8,128)S(1)} %custom-call.7, f32[64,256]{1,0:T(8,128)S(1)} %add.87, f32[64,256]{1,0:T(8,128)} %copy-done.3), kind=kOutput, calls=%fused_computation.19 | convolution fusion | flops 12615680 | bytes 212992 | tf_op jit(solution)/shard_map/jit(_solve_triangular)/triangular_solve | solution.py:56
  43.9 0.7 %collective-permute-done.5 = f32[256,512]{1,0:T(8,128)} collective-permute-done((f32[256,512]{1,0:T(8,128)}, f32[256,512]{1,0:T(8,128)}, u32[]{:S(2)}, u32[]{:S(2)}) %collective-permute-start.5) | collective-permute-done | bytes 524320 | tf_op jit(solution)/shard_map/ppermute | solution.py:52
  44.6 1.5 %convolution_multiply_fusion.1 = f32[64,512]{1,0:T(8,128)S(1)} fusion(f32[64,256]{1,0:T(8,128)S(1)} %fusion.10, f32[256,512]{1,0:T(8,128)} %add.94, f32[256,512]{1,0:T(8,128)} %collective-permute-done.5), kind=kOutput, calls=%fused_computation.2 | convolution fusion | flops 50495488 | bytes 1245184 | tf_op jit(solution)/shard_map/dot_general | solution.py:57
  46.1 0.1 collective-permute-start.6
  46.2 0.0 collective-permute-done.7
  46.2 0.0 collective-permute-done.8
  46.2 0.0 collective-permute-done.9
  46.2 2.0 %add_add_fusion = f32[256,256]{1,0:T(8,128)} fusion(f32[256,256]{1,0:T(8,128)} %collective-permute-done.9, f32[256,256]{1,0:T(8,128)} %collective-permute-done.8, f32[256,256]{1,0:T(8,128)} %collective-permute-done.7, f32[1024,256]{1,0:T(8,128)} %fusion.17, s32[]{:T(128)S(6)} %select_n.60), kind=kLoop, calls=%fused_computation.14 | loop fusion | flops 196608 | bytes 1310724 | tf_op jit(solution)/shard_map/add | solution.py:45
  48.2 0.0 collective-permute-done.6
  48.2 0.0 copy-done.2
  48.2 2.0 %subtract_bitcast_fusion = (f32[1,256,1024]{2,1,0:T(8,128)}, f32[256,1024]{1,0:T(8,128)}) fusion(f32[256,1024]{1,0:T(8,128)S(1)} %fusion, f32[256,1024]{1,0:T(8,128)S(1)} %copy-done.2, f32[64,256]{1,0:T(8,128)S(1)} %fusion.10, f32[64,512]{1,0:T(8,128)S(1)} %collective-permute-done.6, f32[64,512]{1,0:T(8,128)S(1)} %convolution_multiply_fusion.1, pred[]{:T(512)S(6)} %eq.9), kind=kOutput, calls=%fused_computation.4 | convolution fusion | flops 101384192 | bytes 4521985 | tf_op jit(solution)/shard_map/dot_general | solution.py:60
  (3 shorter events, 0.0 us)
Async XLA Ops:
  0.6 1.6 %copy-start = (bf16[1024,1024]{1,0:T(8,128)(2,1)S(1)}, bf16[1024,1024]{1,0:T(8,128)(2,1)}, u32[]{:S(2)}) copy-start(bf16[1024,1024]{1,0:T(8,128)(2,1)} %param.6) | copy-start | bytes 6291460
  2.2 3.5 %copy-start.4 = (f32[1024,64]{0,1:T(8,128)S(1)}, f32[1024,64]{0,1:T(8,128)}, u32[]{:S(2)}) copy-start(f32[1024,64]{0,1:T(8,128)} %param.9) | copy-start | bytes 786436
  4.4 2.0 %copy-start.1 = (f32[256,1024]{1,0:T(8,128)S(1)}, f32[256,1024]{1,0:T(8,128)}, u32[]{:S(2)}) copy-start(f32[256,1024]{1,0:T(8,128)} %param.7) | copy-start | bytes 3145732
  5.2 16.4 %collective-permute-start.3 = (f32[256,512]{1,0:T(8,128)}, f32[256,512]{1,0:T(8,128)}, u32[]{:S(2)}, u32[]{:S(2)}) collective-permute-start(f32[256,512]{1,0:T(8,128)} %constant_dynamic-slice_fusion.3), channel_id=1, source_target_pairs={{0,4},{4,0},{8,12},{12,8},{16,20},{20,16},{24,28},{28,24},{1,5},{5... | collective-permute-start | bytes 1572872 | tf_op jit(solution)/shard_map/ppermute | solution.py:35
  6.3 2.3 %collective-permute-start = (f32[64,256]{1,0:T(8,128)S(1)}, f32[64,256]{1,0:T(8,128)S(1)}, u32[]{:S(2)}, u32[]{:S(2)}) collective-permute-start(f32[64,256]{1,0:T(8,128)S(1)} %convolution_bitcast_fusion), channel_id=1, source_target_pairs={{0,4},{4,0},{8,12},{12,8},{16,20},{20,16},{24,28},{28,24},{1,5},{5... | collective-permute-start | bytes 196616 | tf_op jit(solution)/shard_map/ppermute | solution.py:34
  8.7 10.5 %collective-permute-start.1 = (f32[64,256]{1,0:T(8,128)S(1)}, f32[64,256]{1,0:T(8,128)}, u32[]{:S(2)}, u32[]{:S(2)}) collective-permute-start(f32[64,256]{1,0:T(8,128)S(1)} %add.86), channel_id=1, source_target_pairs={{0,8},{4,12},{8,0},{12,4},{16,24},{20,28},{24,16},{28,20},{1,9},{5... | collective-permute-start | bytes 196616 | tf_op jit(solution)/shard_map/ppermute | solution.py:51
  13.7 32.5 %collective-permute-start.7 = (f32[256,256]{1,0:T(8,128)}, f32[256,256]{1,0:T(8,128)}, u32[]{:S(2)}, u32[]{:S(2)}) collective-permute-start(f32[256,256]{1,0:T(8,128)} %get-tuple-element.3), channel_id=1, source_target_pairs={{0,1},{1,2},{2,3},{3,0},{4,5},{5,6},{6,7},{7,4},{8,9},{9,10},{10,1... | collective-permute-start | bytes 786440 | tf_op jit(solution)/shard_map/ppermute | solution.py:45
  15.3 30.9 %collective-permute-start.8 = (f32[256,256]{1,0:T(8,128)}, f32[256,256]{1,0:T(8,128)}, u32[]{:S(2)}, u32[]{:S(2)}) collective-permute-start(f32[256,256]{1,0:T(8,128)} %get-tuple-element.5), channel_id=1, source_target_pairs={{0,2},{1,3},{2,0},{3,1},{4,6},{5,7},{6,4},{7,5},{8,10},{9,11},{10,... | collective-permute-start | bytes 786440 | tf_op jit(solution)/shard_map/ppermute | solution.py:45
  17.9 28.4 %collective-permute-start.9 = (f32[256,256]{1,0:T(8,128)S(1)}, f32[256,256]{1,0:T(8,128)}, u32[]{:S(2)}, u32[]{:S(2)}) collective-permute-start(f32[256,256]{1,0:T(8,128)S(1)} %get-tuple-element.4), channel_id=1, source_target_pairs={{0,3},{1,0},{2,1},{3,2},{4,7},{5,4},{6,5},{7,6},{8,11},{9,8},{10,9... | collective-permute-start | bytes 786440 | tf_op jit(solution)/shard_map/ppermute | solution.py:45
  20.1 4.3 %collective-permute-start.2 = (f32[64,256]{1,0:T(8,128)S(1)}, f32[64,256]{1,0:T(8,128)S(1)}, u32[]{:S(2)}, u32[]{:S(2)}) collective-permute-start(f32[64,256]{1,0:T(8,128)S(1)} %add.87), channel_id=1, source_target_pairs={{0,16},{4,20},{8,24},{12,28},{16,0},{20,4},{24,8},{28,12},{1,17},{... | collective-permute-start | bytes 196616 | tf_op jit(solution)/shard_map/ppermute | solution.py:51
  23.6 9.5 %collective-permute-start.4 = (f32[256,512]{1,0:T(8,128)}, f32[256,512]{1,0:T(8,128)}, u32[]{:S(2)}, u32[]{:S(2)}) collective-permute-start(f32[256,512]{1,0:T(8,128)} %dynamic-slice_add_fusion), channel_id=1, source_target_pairs={{0,8},{4,20},{8,0},{12,28},{16,24},{20,4},{24,16},{28,12},{1,9},{5... | collective-permute-start | bytes 1572872 | tf_op jit(solution)/shard_map/ppermute | solution.py:52
  24.4 0.6 %copy-start.3 = (f32[64,256]{1,0:T(8,128)}, f32[64,256]{1,0:T(8,128)S(1)}, u32[]{:S(2)}) copy-start(f32[64,256]{1,0:T(8,128)S(1)} %collective-permute-done.2) | copy-start | bytes 196612
  35.1 9.5 %collective-permute-start.5 = (f32[256,512]{1,0:T(8,128)}, f32[256,512]{1,0:T(8,128)}, u32[]{:S(2)}, u32[]{:S(2)}) collective-permute-start(f32[256,512]{1,0:T(8,128)} %add.94), channel_id=1, source_target_pairs={{0,16},{4,12},{8,24},{12,4},{16,0},{20,28},{24,8},{28,20},{1,17},{... | collective-permute-start | bytes 1572872 | tf_op jit(solution)/shard_map/ppermute | solution.py:52
  42.7 5.5 %copy-start.2 = (f32[256,1024]{1,0:T(8,128)S(1)}, f32[256,1024]{1,0:T(8,128)}, u32[]{:S(2)}) copy-start(f32[256,1024]{1,0:T(8,128)} %param.7) | copy-start | bytes 3145732
  46.1 2.1 %collective-permute-start.6 = (f32[64,512]{1,0:T(8,128)S(1)}, f32[64,512]{1,0:T(8,128)S(1)}, u32[]{:S(2)}, u32[]{:S(2)}) collective-permute-start(f32[64,512]{1,0:T(8,128)S(1)} %convolution_multiply_fusion.1), channel_id=1, source_target_pairs={{0,4},{4,0},{8,12},{12,8},{16,20},{20,16},{24,28},{28,24},{1,5},{5... | collective-permute-start | bytes 393224 | tf_op jit(solution)/shard_map/ppermute | solution.py:58

commit v2 on v0

v2 whole, which is shorter than its diff:
```python
import functools
import math

import jax
import jax.numpy as jnp
from jax import lax
from jax.experimental import pallas as pl
from jax.experimental.pallas import tpu as pltpu
from jax.sharding import PartitionSpec as P

F32 = jnp.float32
BF16 = jnp.bfloat16
NN = (((1,), (0,)), ((), ()))
NT = (((1,), (1,)), ((), ()))
VMEM = pl.BlockSpec(memory_space=pltpu.VMEM)
ANY = pl.BlockSpec(memory_space=pl.ANY)
HBM = pl.BlockSpec(memory_space=pltpu.HBM)


def swap(bit_even, bit_odd, size):
    return [(i, i ^ (bit_odd if i & 1 else bit_even)) for i in range(size)]


def split(x):
    high = x.astype(BF16)
    return high, (x - high.astype(F32)).astype(BF16)


def dot(a, b, dims):
    return lax.dot_general(a, b, dims, preferred_element_type=F32)


def dot3(a, b, dims):
    (ah, al), (bh, bl) = split(a), split(b)
    return dot(ah, bh, dims) + (dot(ah, bl, dims) + dot(al, bh, dims))


def front_kernel(chunks, n_tensor, acts, og, wt, err, qt, *rest):
    theirs, mine, left = rest[:3]
    blocks = rest[3 : 3 + n_tensor]
    acts_v, og_v, wt_v, err_v, qt_v, acts_t, part, sems = rest[3 + n_tensor :]
    tok, din = acts.shape
    cols = og.shape[1]
    width = cols // chunks
    half = chunks // 2
    side = lax.rem(lax.axis_index("dp"), 2)
    copies = [pltpu.make_async_copy(acts, acts_v, sems.at[4 * chunks])]
    copies[0].start()
    for c in range(chunks):
        at = pl.multiple_of(lax.rem((1 - side) * half + c, chunks) * width, width)
        span = pl.ds(at, width)
        group = [
            pltpu.make_async_copy(og.at[:, span], og_v.at[c], sems.at[4 * c]),
            pltpu.make_async_copy(err.at[0, :, span], err_v.at[c], sems.at[4 * c + 1]),
            pltpu.make_async_copy(qt.at[:, span], qt_v.at[c], sems.at[4 * c + 2]),
            pltpu.make_async_copy(wt.at[:, span], wt_v.at[c], sems.at[4 * c + 3]),
        ]
        for one in group:
            one.start()
        copies.append(group)
    copies[0].wait()
    acts_t[...] = acts_v[...].T
    scale = 1.0 / math.sqrt(tok)
    for c in range(chunks):
        group = copies[1 + c]
        group[0].wait()
        grad = dot(acts_t[...], og_v[c], NN)
        group[1].wait()
        merged = grad * scale + err_v[c]
        out = theirs if c < half else mine
        out[:, (c % half) * width : (c % half + 1) * width] = merged
        group[2].wait()
        add = dot3(qt_v[c], merged, NT)
        if c == 0:
            left[...] = add
        else:
            left[...] += add
        group[3].wait()
        high, low = split(wt_v[c])
        add = dot(og_v[c], high, NT) + dot(og_v[c], low, NT)
        if c == 0:
            part[...] = add
        elif c < chunks - 1:
            part[...] += add
        else:
            part[...] += add
    me = lax.axis_index("tensor")
    block = tok // n_tensor
    for k in range(n_tensor):
        at = pl.multiple_of(lax.rem(me + k, n_tensor) * block, block)
        blocks[k][...] = part[pl.ds(at, block), :]


def front(acts, og, wt, err, qt, n_tensor):
    tok, din = acts.shape
    cols = og.shape[1]
    rank = qt.shape[0]
    chunks = 4 if cols % 512 == 0 else 2
    width = cols // chunks
    shape = jax.ShapeDtypeStruct
    return pl.pallas_call(
        functools.partial(front_kernel, chunks, n_tensor),
        out_shape=[shape((din, cols // 2), F32)] * 2
        + [shape((rank, din), F32)]
        + [shape((tok // n_tensor, din), F32)] * n_tensor,
        in_specs=[HBM] * 5,
        out_specs=[VMEM] * (3 + n_tensor),
        scratch_shapes=[
            pltpu.VMEM((tok, din), BF16),
            pltpu.VMEM((chunks, tok, width), BF16),
            pltpu.VMEM((chunks, din, width), F32),
            pltpu.VMEM((chunks, din, width), F32),
            pltpu.VMEM((chunks, rank, width), F32),
            pltpu.VMEM((din, tok), BF16),
            pltpu.VMEM((tok, din), F32),
            pltpu.SemaphoreType.DMA((4 * chunks + 1,)),
        ],
        compiler_params=pltpu.CompilerParams(vmem_limit_bytes=24 << 20),
        cost_estimate=pl.CostEstimate(
            flops=6 * tok * din * cols, bytes_accessed=5 << 20, transcendentals=0
        ),
        name="front",
    )(acts, og, wt, err, qt)


def ortho_kernel(replicas, a_ref, b_ref, o_ref):
    left = (a_ref[...] + b_ref[...]) * (1.0 / replicas)
    rank, din = left.shape
    gram = lax.dot_general(
        left, left, NT, precision=lax.Precision.HIGHEST, preferred_element_type=F32
    )
    tiles = rank // 8
    gs = [gram[8 * i : 8 * i + 8, :] for i in range(tiles)]
    ls = [left[8 * i : 8 * i + 8, :] for i in range(tiles)]
    for k in range(rank):
        i, s = divmod(k, 8)
        columns = [jnp.broadcast_to(g[:, k : k + 1], (8, din)) for g in gs[i:]]
        pivot = columns[0][s : s + 1, :]
        inverse = 1.0 / pivot
        row_g = gs[i][s : s + 1, :]
        row_l = ls[i][s : s + 1, :]
        o_ref[k : k + 1, :] = row_l * lax.rsqrt(pivot)
        if k == rank - 1:
            break
        step_g = row_g * inverse[:, :rank]
        step_l = row_l * inverse
        for j in range(i, tiles):
            gs[j] = gs[j] - columns[j - i][:, :rank] * step_g
            ls[j] = ls[j] - columns[j - i] * step_l


def ortho_of(a, b, replicas):
    rank, din = a.shape
    return pl.pallas_call(
        functools.partial(ortho_kernel, replicas),
        out_shape=jax.ShapeDtypeStruct((rank, din), F32),
        in_specs=[VMEM] * 2,
        out_specs=VMEM,
        compiler_params=pltpu.CompilerParams(vmem_limit_bytes=4 << 20),
        cost_estimate=pl.CostEstimate(
            flops=1 << 30, bytes_accessed=1 << 20, transcendentals=0
        ),
        name="ortho",
    )(a, b)


def right_kernel(replicas, o_ref, a_ref, b_ref, r_ref):
    r_ref[...] = dot3(o_ref[...], a_ref[...] + b_ref[...], NN) * (1.0 / replicas)


def right_of(ortho, a, b, replicas):
    return pl.pallas_call(
        functools.partial(right_kernel, replicas),
        out_shape=jax.ShapeDtypeStruct((ortho.shape[0], a.shape[1]), F32),
        in_specs=[VMEM] * 3,
        out_specs=VMEM,
        compiler_params=pltpu.CompilerParams(vmem_limit_bytes=8 << 20),
        name="right",
    )(ortho, a, b)


def back_kernel(chunks, o_ref, mine_r, theirs_r, mine, theirs, wt, new_w, new_e, wv, ev, sems):
    cols = wt.shape[1]
    width = cols // chunks
    half = chunks // 2
    side = lax.rem(lax.axis_index("dp"), 2)
    flipped = o_ref[...].T
    copies = []
    for c in range(chunks):
        at = pl.multiple_of(lax.rem(side * half + c, chunks) * width, width)
        here = slice((c % half) * width, (c % half + 1) * width)
        right, merged = (mine_r, mine) if c < half else (theirs_r, theirs)
        delta = dot3(flipped, right[:, here], NN)
        ev[c] = merged[:, here] - delta
        wv[c] = wt[:, pl.ds(at, width)] - delta
        for one in (
            pltpu.make_async_copy(ev.at[c], new_e.at[0, :, pl.ds(at, width)], sems.at[2 * c]),
            pltpu.make_async_copy(wv.at[c], new_w.at[:, pl.ds(at, width)], sems.at[2 * c + 1]),
        ):
            one.start()
            copies.append(one)
    for one in copies:
        one.wait()


def back(ortho, mine_r, theirs_r, mine, theirs, wt):
    din, cols = wt.shape
    chunks = 4 if cols % 512 == 0 else 2
    width = cols // chunks
    return pl.pallas_call(
        functools.partial(back_kernel, chunks),
        out_shape=[
            jax.ShapeDtypeStruct((din, cols), F32),
            jax.ShapeDtypeStruct((1, din, cols), F32),
        ],
        in_specs=[VMEM] * 6,
        out_specs=[ANY] * 2,
        scratch_shapes=[
            pltpu.VMEM((chunks, din, width), F32),
            pltpu.VMEM((chunks, din, width), F32),
            pltpu.SemaphoreType.DMA((2 * chunks,)),
        ],
        compiler_params=pltpu.CompilerParams(vmem_limit_bytes=16 << 20),
        name="back",
    )(ortho, mine_r, theirs_r, mine, theirs, wt)


def local(acts, out_grad, weight, error, start_q):
    replicas = lax.axis_size("dp")
    n_tensor = lax.axis_size("tensor")
    bits = [1 << b for b in range(1, replicas.bit_length() - 1)]
    pair = swap(1, 1, replicas)

    theirs, mine, left, *blocks = front(
        acts, out_grad, weight, error, start_q.T, n_tensor
    )
    total = mine + lax.ppermute(theirs, "dp", pair)
    left = left + lax.ppermute(left, "dp", pair)
    input_grad = blocks[0]
    for k in range(1, n_tensor):
        hop = [(i, (i + k) % n_tensor) for i in range(n_tensor)]
        input_grad = input_grad + lax.ppermute(blocks[k], "tensor", hop)

    for even, odd in zip(bits[:-1], bits[:0:-1]):
        total = total + lax.ppermute(total, "dp", swap(even, odd, replicas))
        left = left + lax.ppermute(left, "dp", swap(even, even, replicas))
    last_total = lax.ppermute(total, "dp", swap(bits[-1], bits[0], replicas))
    last_left = lax.ppermute(left, "dp", swap(bits[-1], bits[-1], replicas))
    ortho = ortho_of(left, last_left, replicas)
    right = right_of(ortho, total, last_total, replicas)
    other = lax.ppermute(right, "dp", pair)
    new_weight, new_error = back(ortho, right, other, mine, theirs, weight)
    return (new_weight, new_error, input_grad)


def solution(mesh):
    placed = (
        P("dp", None),
        P("dp", "tensor"),
        P(None, "tensor"),
        P("dp", None, "tensor"),
        P("tensor", None),
    )
    return jax.shard_map(
        local,
        mesh=mesh,
        in_specs=placed,
        out_specs=(P(None, "tensor"), P("dp", None, "tensor"), P(("dp", "tensor"), None)),
        check_vma=False,
    )
```

time: 153 us -> 55.7 us (0.36)
  the two profiles are of different devices: /device:TPU:0 before, /device:TPU:11 now
where the time goes in v2:
time: 55.7 us; the launch traced here: 55.4 us
  waiting for transfers between devices  21.8 us (39%)
  Pallas kernels  14.1 us (25%)
  starting transfers between devices  11.9 us (21%)
  local copies, waits for them, and re-layouts  6.02 us (11%)
  other arithmetic  0.95 us (2%)
  between operations  0.68 us (1%)
    ppermute x1, waiting for transfers between devices, local(): total = total + lax.ppermute(total, 'dp', swap(even, odd, replicas))  7.09 us
    ppermute x3, waiting for transfers between devices, local(): input_grad = input_grad + lax.ppermute(blocks[k], 'tensor', hop)  6.86 us
    pallas_call x1, Pallas kernels, front(): pl.pallas_call(functools.partial(front_kernel, chunks, n_tensor), out_sha...  6.52 us
    unnamed x10, local copies, waits for them, and re-layouts  6.02 us
    pallas_call x1, Pallas kernels, ortho_of(): pl.pallas_call(functools.partial(ortho_kernel, replicas), out_shape=jax.S...  5.42 us
    ppermute x3, starting transfers between devices, local(): input_grad = input_grad + lax.ppermute(blocks[k], 'tensor', hop)  3.78 us
    ppermute x1, waiting for transfers between devices, local(): last_left = lax.ppermute(left, 'dp', swap(bits[-1], bits[-1], replicas))  3.17 us
    ppermute x1, waiting for transfers between devices, local(): left = left + lax.ppermute(left, 'dp', swap(even, even, replicas))  3.16 us
  transfers between devices with their start and end apart: 10, of which 6 were waited for; matrix products, arithmetic and copies ran while one was open for 1% of the time, Pallas kernels for 10%

profile of v2, /device:TPU:11, one launch (start us, length us, event | category | flops | bytes accessed | tf_op | source)
XLA Modules:
  0.0 55.4 jit_solution(4132806797054288254)
XLA Ops:
  0.6 0.0 copy-start
  0.6 1.2 %copy-done = f32[256,1024]{1,0:T(8,128)S(1)} copy-done((f32[256,1024]{1,0:T(8,128)S(1)}, f32[256,1024]{1,0:T(8,128)}, u32[]{:S(2)}) %copy-start) | copy-done | bytes 1048600
  1.9 0.0 copy-start.1
  1.9 1.6 %copy-done.1 = bf16[1024,1024]{1,0:T(8,128)(2,1)S(1)} copy-done((bf16[1024,1024]{1,0:T(8,128)(2,1)S(1)}, bf16[1024,1024]{1,0:T(8,128)(2,1)}, u32[]{:S(2)}) %copy-start.1) | copy-done | bytes 2097176
  3.4 0.0 copy-start.2
  3.5 1.2 %copy-done.2 = f32[1,256,1024]{2,1,0:T(8,128)S(1)} copy-done((f32[1,256,1024]{2,1,0:T(8,128)S(1)}, f32[1,256,1024]{2,1,0:T(8,128)}, u32[]{:S(2)}) %copy-start.2) | copy-done | bytes 1048600
  4.7 0.0 copy-start.3
  4.7 1.0 %copy-done.3 = bf16[1024,256]{1,0:T(8,128)(2,1)S(1)} copy-done((bf16[1024,256]{1,0:T(8,128)(2,1)S(1)}, bf16[1024,256]{1,0:T(8,128)(2,1)}, u32[]{:S(2)}) %copy-start.3) | copy-done | bytes 524312
  5.7 0.0 copy-start.4
  5.7 0.9 %copy-done.4 = f32[1024,64]{0,1:T(8,128)S(1)} copy-done((f32[1024,64]{0,1:T(8,128)S(1)}, f32[1024,64]{0,1:T(8,128)}, u32[]{:S(2)}) %copy-start.4) | copy-done | bytes 262168
  6.7 6.5 %front.1 = (f32[256,512]{1,0:T(8,128)S(1)}, f32[256,512]{1,0:T(8,128)S(1)}, f32[64,256]{1,0:T(8,128)S(1)}, f32[256,256]{1,0:T(8,128)S(1)}, f32[256,256]{1,0:T(8,...) custom-call(bf16[1024,256]{1,0:T(8,128)(2,1)S(1)} %copy-done.3, bf16[1024,1024]{1,0:T(8,128)(2,1)S(1)} %copy-done.1, ...), custom_call_target="tpu_custom_call" | custom-call | flops 1610612736 | bytes 5242880 | tf_op jit(solution)/shard_map/front/pallas_call | solution.py:101
  13.2 0.7 %collective-permute-start.3 = (f32[256,512]{1,0:T(8,128)S(1)}, f32[256,512]{1,0:T(8,128)S(1)}, u32[]{:S(2)}, u32[]{:S(2)}) collective-permute-start(f32[256,512]{1,0:T(8,128)S(1)} %get-tuple-element.14.theirs), channel_id=1, source_target_pairs={{0,4},{4,0},{8,12},{12,8},{16,20},{20,16},{24,28},{28,24},{1,5},{5... | collective-permute-start | bytes 1572872 | tf_op jit(solution)/shard_map/ppermute | solution.py:237
  13.9 1.5 %collective-permute-done.3 = f32[256,512]{1,0:T(8,128)S(1)} collective-permute-done((f32[256,512]{1,0:T(8,128)S(1)}, f32[256,512]{1,0:T(8,128)S(1)}, u32[]{:S(2)}, u32[]{:S(2)}) %collective-permute-start.3) | collective-permute-done | bytes 524320 | tf_op jit(solution)/shard_map/ppermute | solution.py:237
  15.5 0.1 add.23
  15.6 1.3 %collective-permute-start.4 = (f32[256,512]{1,0:T(8,128)S(1)}, f32[256,512]{1,0:T(8,128)S(1)}, u32[]{:S(2)}, u32[]{:S(2)}) collective-permute-start(f32[256,512]{1,0:T(8,128)S(1)} %add.23), channel_id=1, source_target_pairs={{0,8},{4,20},{8,0},{12,28},{16,24},{20,4},{24,16},{28,12},{1,9},{5... | collective-permute-start | bytes 1572872 | tf_op jit(solution)/shard_map/ppermute | solution.py:245
  16.9 7.1 %collective-permute-done.4 = f32[256,512]{1,0:T(8,128)S(1)} collective-permute-done((f32[256,512]{1,0:T(8,128)S(1)}, f32[256,512]{1,0:T(8,128)S(1)}, u32[]{:S(2)}, u32[]{:S(2)}) %collective-permute-start.4) | collective-permute-done | bytes 524320 | tf_op jit(solution)/shard_map/ppermute | solution.py:245
  23.9 0.1 add.24.a_ref
  24.0 0.3 collective-permute-start.5
  24.4 2.5 %collective-permute-start = (f32[64,256]{1,0:T(8,128)S(1)}, f32[64,256]{1,0:T(8,128)S(1)}, u32[]{:S(2)}, u32[]{:S(2)}) collective-permute-start(f32[64,256]{1,0:T(8,128)S(1)} %get-tuple-element.12), channel_id=1, source_target_pairs={{0,4},{4,0},{8,12},{12,8},{16,20},{20,16},{24,28},{28,24},{1,5},{5... | collective-permute-start | bytes 196616 | tf_op jit(solution)/shard_map/ppermute | solution.py:238
  26.8 1.3 %collective-permute-start.7 = (f32[256,256]{1,0:T(8,128)S(1)}, f32[256,256]{1,0:T(8,128)S(1)}, u32[]{:S(2)}, u32[]{:S(2)}) collective-permute-start(f32[256,256]{1,0:T(8,128)S(1)} %get-tuple-element.18), channel_id=1, source_target_pairs={{0,1},{1,2},{2,3},{3,0},{4,5},{5,6},{6,7},{7,4},{8,9},{9,10},{10,1... | collective-permute-start | bytes 786440 | tf_op jit(solution)/shard_map/ppermute | solution.py:242
  28.1 1.0 %collective-permute-start.8 = (f32[256,256]{1,0:T(8,128)S(1)}, f32[256,256]{1,0:T(8,128)S(1)}, u32[]{:S(2)}, u32[]{:S(2)}) collective-permute-start(f32[256,256]{1,0:T(8,128)S(1)} %get-tuple-element.19), channel_id=1, source_target_pairs={{0,2},{1,3},{2,0},{3,1},{4,6},{5,7},{6,4},{7,5},{8,10},{9,11},{10,... | collective-permute-start | bytes 786440 | tf_op jit(solution)/shard_map/ppermute | solution.py:242
  29.2 1.5 %collective-permute-start.9 = (f32[256,256]{1,0:T(8,128)S(1)}, f32[256,256]{1,0:T(8,128)S(1)}, u32[]{:S(2)}, u32[]{:S(2)}) collective-permute-start(f32[256,256]{1,0:T(8,128)S(1)} %get-tuple-element.20), channel_id=1, source_target_pairs={{0,3},{1,0},{2,1},{3,2},{4,7},{5,4},{6,5},{7,6},{8,11},{9,8},{10,9... | collective-permute-start | bytes 786440 | tf_op jit(solution)/shard_map/ppermute | solution.py:242
  30.6 0.0 collective-permute-done
  30.6 0.3 collective-permute-start.1
  31.0 3.2 %collective-permute-done.1 = f32[64,256]{1,0:T(8,128)S(1)} collective-permute-done((f32[64,256]{1,0:T(8,128)S(1)}, f32[64,256]{1,0:T(8,128)S(1)}, u32[]{:S(2)}, u32[]{:S(2)}) %collective-permute-start.1) | collective-permute-done | bytes 65568 | tf_op jit(solution)/shard_map/ppermute | solution.py:246
  34.1 0.3 collective-permute-start.2
  34.4 3.2 %collective-permute-done.2.b_ref = f32[64,256]{1,0:T(8,128)S(1)} collective-permute-done((f32[64,256]{1,0:T(8,128)S(1)}, f32[64,256]{1,0:T(8,128)S(1)}, u32[]{:S(2)}, u32[]{:S(2)}) %collective-permute-start.2) | collective-permute-done | bytes 65568 | tf_op jit(solution)/shard_map/ppermute | solution.py:248
  37.6 5.4 %ortho.1.o_ref = f32[64,256]{1,0:T(8,128)S(1)} custom-call(f32[64,256]{1,0:T(8,128)S(1)} %add.22.a_ref, f32[64,256]{1,0:T(8,128)S(1)} %collective-permute-done.2.b_ref), custom_call_target="tpu_custom_call" | custom-call | flops 1073741824 | bytes 1048576 | tf_op jit(solution)/shard_map/ortho/pallas_call | solution.py:154
  43.0 0.0 collective-permute-done.5.b_ref
  43.0 0.3 right.1.mine_r
  43.4 2.6 %collective-permute-start.6 = (f32[64,512]{1,0:T(8,128)S(1)}, f32[64,512]{1,0:T(8,128)S(1)}, u32[]{:S(2)}, u32[]{:S(2)}) collective-permute-start(f32[64,512]{1,0:T(8,128)S(1)} %right.1.mine_r), channel_id=1, source_target_pairs={{0,4},{4,0},{8,12},{12,8},{16,20},{20,16},{24,28},{28,24},{1,5},{5... | collective-permute-start | bytes 393224 | tf_op jit(solution)/shard_map/ppermute | solution.py:251
  46.0 0.0 collective-permute-done.7
  46.0 4.7 %collective-permute-done.8 = f32[256,256]{1,0:T(8,128)S(1)} collective-permute-done((f32[256,256]{1,0:T(8,128)S(1)}, f32[256,256]{1,0:T(8,128)S(1)}, u32[]{:S(2)}, u32[]{:S(2)}) %collective-permute-start.8) | collective-permute-done | bytes 262176 | tf_op jit(solution)/shard_map/ppermute | solution.py:242
  50.7 2.2 %collective-permute-done.9 = f32[256,256]{1,0:T(8,128)S(1)} collective-permute-done((f32[256,256]{1,0:T(8,128)S(1)}, f32[256,256]{1,0:T(8,128)S(1)}, u32[]{:S(2)}, u32[]{:S(2)}) %collective-permute-start.9) | collective-permute-done | bytes 262176 | tf_op jit(solution)/shard_map/ppermute | solution.py:242
  52.8 0.8 %add_add_fusion = f32[256,256]{1,0:T(8,128)} fusion(f32[256,256]{1,0:T(8,128)S(1)} %collective-permute-done.9, f32[256,256]{1,0:T(8,128)S(1)} %collective-permute-done.8, f32[256,256]{1,0:T(8,128)S(1)} %get-tuple-element.17, f32[256,256]{1,0:T(8,128)S(1)} %collective-permute-done.7), kind=kLoop, calls=%fused_computation | loop fusion | flops 196608 | bytes 1310720 | tf_op jit(solution)/shard_map/add | solution.py:242
  53.6 0.0 collective-permute-done.6.theirs_r
  53.6 1.8 %back.1 = (f32[256,1024]{1,0:T(8,128)}, f32[1,256,1024]{2,1,0:T(8,128)}) custom-call(f32[64,256]{1,0:T(8,128)S(1)} %ortho.1.o_ref, f32[64,512]{1,0:T(8,128)S(1)} %right.1.mine_r, f32[64,512]{1,0:T(8,128)S(1)} %collective-permute-done.6.theirs_r, f32[256,512]{1,0:T(8,128)S(1)} %get-tuple-element.13.mine, f32[256,512]{1,0:T(8,128)S(1)} %get-tuple-element.14.theirs, ...), custom_call_target="tpu_custom_call" | custom-call | tf_op jit(solution)/shard_map/back/pallas_call | solution.py:210
  (2 shorter events, 0.0 us)
Async XLA Ops:
  0.6 1.2 %copy-start = (f32[256,1024]{1,0:T(8,128)S(1)}, f32[256,1024]{1,0:T(8,128)}, u32[]{:S(2)}) copy-start(f32[256,1024]{1,0:T(8,128)} %wt.3) | copy-start | bytes 3145732
  1.9 1.6 %copy-start.1 = (bf16[1024,1024]{1,0:T(8,128)(2,1)S(1)}, bf16[1024,1024]{1,0:T(8,128)(2,1)}, u32[]{:S(2)}) copy-start(bf16[1024,1024]{1,0:T(8,128)(2,1)} %og.1) | copy-start | bytes 6291460
  3.4 1.2 %copy-start.2 = (f32[1,256,1024]{2,1,0:T(8,128)S(1)}, f32[1,256,1024]{2,1,0:T(8,128)}, u32[]{:S(2)}) copy-start(f32[1,256,1024]{2,1,0:T(8,128)} %err.1) | copy-start | bytes 3145732
  4.7 1.0 %copy-start.3 = (bf16[1024,256]{1,0:T(8,128)(2,1)S(1)}, bf16[1024,256]{1,0:T(8,128)(2,1)}, u32[]{:S(2)}) copy-start(bf16[1024,256]{1,0:T(8,128)(2,1)} %acts.1) | copy-start | bytes 1572868
  5.7 0.9 %copy-start.4 = (f32[1024,64]{0,1:T(8,128)S(1)}, f32[1024,64]{0,1:T(8,128)}, u32[]{:S(2)}) copy-start(f32[1024,64]{0,1:T(8,128)} %param.9) | copy-start | bytes 786436
  13.2 2.3 %collective-permute-start.3 = (f32[256,512]{1,0:T(8,128)S(1)}, f32[256,512]{1,0:T(8,128)S(1)}, u32[]{:S(2)}, u32[]{:S(2)}) collective-permute-start(f32[256,512]{1,0:T(8,128)S(1)} %get-tuple-element.14.theirs), channel_id=1, source_target_pairs={{0,4},{4,0},{8,12},{12,8},{16,20},{20,16},{24,28},{28,24},{1,5},{5... | collective-permute-start | bytes 1572872 | tf_op jit(solution)/shard_map/ppermute | solution.py:237
  15.6 8.4 %collective-permute-start.4 = (f32[256,512]{1,0:T(8,128)S(1)}, f32[256,512]{1,0:T(8,128)S(1)}, u32[]{:S(2)}, u32[]{:S(2)}) collective-permute-start(f32[256,512]{1,0:T(8,128)S(1)} %add.23), channel_id=1, source_target_pairs={{0,8},{4,20},{8,0},{12,28},{16,24},{20,4},{24,16},{28,12},{1,9},{5... | collective-permute-start | bytes 1572872 | tf_op jit(solution)/shard_map/ppermute | solution.py:245
  24.0 19.0 %collective-permute-start.5 = (f32[256,512]{1,0:T(8,128)S(1)}, f32[256,512]{1,0:T(8,128)S(1)}, u32[]{:S(2)}, u32[]{:S(2)}) collective-permute-start(f32[256,512]{1,0:T(8,128)S(1)} %add.24.a_ref), channel_id=1, source_target_pairs={{0,16},{4,12},{8,24},{12,4},{16,0},{20,28},{24,8},{28,20},{1,17},{... | collective-permute-start | bytes 1572872 | tf_op jit(solution)/shard_map/ppermute | solution.py:247
  24.4 6.3 %collective-permute-start = (f32[64,256]{1,0:T(8,128)S(1)}, f32[64,256]{1,0:T(8,128)S(1)}, u32[]{:S(2)}, u32[]{:S(2)}) collective-permute-start(f32[64,256]{1,0:T(8,128)S(1)} %get-tuple-element.12), channel_id=1, source_target_pairs={{0,4},{4,0},{8,12},{12,8},{16,20},{20,16},{24,28},{28,24},{1,5},{5... | collective-permute-start | bytes 196616 | tf_op jit(solution)/shard_map/ppermute | solution.py:238
  26.8 19.1 %collective-permute-start.7 = (f32[256,256]{1,0:T(8,128)S(1)}, f32[256,256]{1,0:T(8,128)S(1)}, u32[]{:S(2)}, u32[]{:S(2)}) collective-permute-start(f32[256,256]{1,0:T(8,128)S(1)} %get-tuple-element.18), channel_id=1, source_target_pairs={{0,1},{1,2},{2,3},{3,0},{4,5},{5,6},{6,7},{7,4},{8,9},{9,10},{10,1... | collective-permute-start | bytes 786440 | tf_op jit(solution)/shard_map/ppermute | solution.py:242
  28.1 22.5 %collective-permute-start.8 = (f32[256,256]{1,0:T(8,128)S(1)}, f32[256,256]{1,0:T(8,128)S(1)}, u32[]{:S(2)}, u32[]{:S(2)}) collective-permute-start(f32[256,256]{1,0:T(8,128)S(1)} %get-tuple-element.19), channel_id=1, source_target_pairs={{0,2},{1,3},{2,0},{3,1},{4,6},{5,7},{6,4},{7,5},{8,10},{9,11},{10,... | collective-permute-start | bytes 786440 | tf_op jit(solution)/shard_map/ppermute | solution.py:242
  29.2 23.7 %collective-permute-start.9 = (f32[256,256]{1,0:T(8,128)S(1)}, f32[256,256]{1,0:T(8,128)S(1)}, u32[]{:S(2)}, u32[]{:S(2)}) collective-permute-start(f32[256,256]{1,0:T(8,128)S(1)} %get-tuple-element.20), channel_id=1, source_target_pairs={{0,3},{1,0},{2,1},{3,2},{4,7},{5,4},{6,5},{7,6},{8,11},{9,8},{10,9... | collective-permute-start | bytes 786440 | tf_op jit(solution)/shard_map/ppermute | solution.py:242
  30.6 3.5 %collective-permute-start.1 = (f32[64,256]{1,0:T(8,128)S(1)}, f32[64,256]{1,0:T(8,128)S(1)}, u32[]{:S(2)}, u32[]{:S(2)}) collective-permute-start(f32[64,256]{1,0:T(8,128)S(1)} %add.21), channel_id=1, source_target_pairs={{0,8},{4,12},{8,0},{12,4},{16,24},{20,28},{24,16},{28,20},{1,9},{5... | collective-permute-start | bytes 196616 | tf_op jit(solution)/shard_map/ppermute | solution.py:246
  34.1 3.5 %collective-permute-start.2 = (f32[64,256]{1,0:T(8,128)S(1)}, f32[64,256]{1,0:T(8,128)S(1)}, u32[]{:S(2)}, u32[]{:S(2)}) collective-permute-start(f32[64,256]{1,0:T(8,128)S(1)} %add.22.a_ref), channel_id=1, source_target_pairs={{0,16},{4,20},{8,24},{12,28},{16,0},{20,4},{24,8},{28,12},{1,17},{... | collective-permute-start | bytes 196616 | tf_op jit(solution)/shard_map/ppermute | solution.py:248
  43.4 10.3 %collective-permute-start.6 = (f32[64,512]{1,0:T(8,128)S(1)}, f32[64,512]{1,0:T(8,128)S(1)}, u32[]{:S(2)}, u32[]{:S(2)}) collective-permute-start(f32[64,512]{1,0:T(8,128)S(1)} %right.1.mine_r), channel_id=1, source_target_pairs={{0,4},{4,0},{8,12},{12,8},{16,20},{20,16},{24,28},{28,24},{1,5},{5... | collective-permute-start | bytes 393224 | tf_op jit(solution)/shard_map/ppermute | solution.py:251
